TPU v7x, 128 devices: a whole 4x4x4 slice. The times are simulated.
128 devices in a mesh: gx: 4 (over y), gy: 32 (over x, z, core).
Axes of the slice: x: 4, y: 4, z: 4, core: 2. Of those that a mesh axis runs over, the one named last changes fastest.
Arguments:
- features: bfloat16 [4, 32, 32, 8, 8, 512], P('gx', 'gy'), may hold values from -6 to 6
- occupancy: int32 [4, 32, 32, 25], P('gx', 'gy'), may hold values from 0 to 2097151, as said below
- neighbors: int32 [4, 32, 32, 27], P('gx', 'gy'), may hold values from 0 to 48, as said below
- face_lists: int32 [4, 32, 8], P('gx', 'gy'), may hold values from 0 to 31, as said below
- face_relays: int32 [4, 32, 8], P('gx', 'gy'), may hold values from 0 to 39, as said below
- send_slots: int32 [4, 32, 32, 1], P('gx', 'gy'), may hold values from -1 to 31, as said below
- receive_order: int32 [4, 32, 16], P('gx', 'gy'), may hold values from 0 to 31, as said below
- weights: bfloat16 [27, 64, 64], replicated, may hold values from -0.15625 to 0.15625
- channel_bias: float32 [64], replicated, may hold values from -3 to 3
Outputs:
- conv_out: bfloat16 [4, 32, 16, 8, 8, 512], P('gx', 'gy')
Inputs may be any that keep to these rules, and one draw needn't show every extreme that they name: `occupancy`: bit k of word w of a held block is voxel 21 * w + k; bits past voxel 8 * 8 * 8 - 1 are zero; slots that hold no block have all words zero. `neighbors`: entries name pool blocks: held slots below 32, then blocks received across faces, then the zero block 48; entry 13 is the block's own slot; other held entries name occupied slots, or any slot where the device holds none. `face_lists`: entries name slots of the device that hold blocks, or any slot where the device holds none. `face_relays`: entries below 32 name occupied held slots, or any slot where the device holds none; the others name blocks received from gy neighbours. `send_slots`: device d of a gx index sends the same number c_d of items, 0 or more, to every device of that gx index, in items q < c_d, and -1 in the others; every occupied held slot is sent exactly once; in every gx index some device has c_d = 1. `receive_order`: every device receives exactly 16 used items; its rows name each of them exactly once.
All inputs are finite; a program needn't handle non-finite values.
Results may differ from a plain program's by a relative error of at most 0.001.
Values may be sent and summed in bfloat16 or wider, within the bound.
A program may use at most 128 MiB of HBM per device.

v0:
```python
import jax
import jax.numpy as jnp
from jax import lax
from jax.experimental import pallas as pl
from jax.experimental.pallas import tpu as pltpu
from jax.sharding import PartitionSpec as P

C = 64
BS = 8
LANES = BS * C
HELD = 32
FACE = 4
OUT = 16
POOL = 49
BATCH = 8
WORD_BITS = 21
MESH = pl.DeviceIdType.MESH
F32 = jnp.float32
BF16 = jnp.bfloat16


def iota(shape, dim):
    return lax.broadcasted_iota(jnp.int32, shape, dim)


def occupancy_bits(words):
    slots, width = words.shape
    voxels = BS**3
    chunks = jnp.concatenate([words & 127, (words >> 7) & 127, words >> 14], axis=0)
    voxel = iota((width, voxels), 1)
    pick = ((voxel * 3121) >> 16) == iota((width, voxels), 0)
    picked = jnp.dot(
        chunks.astype(F32).astype(BF16),
        jnp.where(pick, 1.0, 0.0).astype(BF16),
        preferred_element_type=F32,
    ).astype(jnp.int32)
    v = iota((slots, voxels), 1)
    bit = v - WORD_BITS * ((v * 3121) >> 16)
    low, mid, high = picked[:slots], picked[slots : 2 * slots], picked[2 * slots :]
    chunk = jnp.where(bit < 7, low, jnp.where(bit < 14, mid, high))
    shift = bit - jnp.where(bit >= 7, 7, 0) - jnp.where(bit >= 14, 7, 0)
    return ((chunk >> shift) & 1).astype(F32)


def build_bands(w_ref, bands):
    zero = jnp.zeros((C, C), BF16)
    for d in range(3):
        for a in range(3):
            taps = [w_ref[9 * a + 3 * d + c] for c in range(3)]
            for k, rz in enumerate((1, 0, 3, 2)):
                left = taps[rz] if rz <= 2 else zero
                right = taps[rz - 1] if rz >= 1 else zero
                pair = jnp.concatenate([left, right], axis=1)
                for xo in range(2):
                    bands[d, pl.ds((a + xo) * 4 * C + k * C, C), xo * 2 * C : (xo + 1) * 2 * C] = pair
        blank = jnp.zeros((4 * C, 2 * C), BF16)
        bands[d, 0 : 4 * C, 2 * C : 4 * C] = blank
        bands[d, 12 * C : 16 * C, 0 : 2 * C] = blank


def kernel(
    face_ref, relay_ref, send_ref, order_ref, nbr_ref, occ_ref, feat_ref, w_ref, bias_ref,
    out_ref,
    raw, pool, mask, bits, tiles, bands, outbox, inbox, fs_y, fr_y, fs_x, fr_x,
    raw_sem, ys, yr, xs, xr, ss, rs,
):
    gx = lax.axis_index("gx")
    gy = lax.axis_index("gy")
    n_gx = lax.axis_size("gx")
    n_gy = lax.axis_size("gy")
    up_y, down_y = lax.rem(gy + 1, n_gy), lax.rem(gy + n_gy - 1, n_gy)
    up_x, down_x = lax.rem(gx + 1, n_gx), lax.rem(gx + n_gx - 1, n_gx)

    barrier = pltpu.get_barrier_semaphore()

    def greet(k, carry):
        pl.semaphore_signal(barrier, inc=1, device_id=(gx, lax.rem(gy + k, n_gy)), device_id_type=MESH)
        return carry

    lax.fori_loop(1, n_gy, greet, 0)
    for other in (up_x, down_x):
        pl.semaphore_signal(barrier, inc=1, device_id=(other, gy), device_id_type=MESH)

    loads = []
    for g in range(4):
        load = pltpu.make_async_copy(feat_ref.at[pl.ds(8 * g, 8)], raw.at[pl.ds(8 * g, 8)], raw_sem.at[g])
        load.start()
        loads.append(load)

    bits[...] = occupancy_bits(occ_ref[...])
    rows = BS * BS
    own_row = jnp.where((iota((rows, LANES), 1) >> 3) == iota((rows, LANES), 0), 1.0, 0.0)
    spread = jnp.where((iota((LANES, LANES), 0) & 7) == (iota((LANES, LANES), 1) >> 6), 1.0, 0.0).astype(BF16)

    def mask_group(g, carry):
        picked = jnp.concatenate([bits[pl.ds(4 * g + i, 1), :] * own_row for i in range(4)], axis=0)
        wide = jnp.dot(picked.astype(BF16), spread, preferred_element_type=F32)
        wide = wide.reshape(4, BS, BS, LANES)
        mask[pl.ds(4 * g, 4)] = wide
        pool[pl.ds(4 * g, 4)] = raw[pl.ds(4 * g, 4)].astype(F32) * wide
        return carry

    for load in loads:
        load.wait()
    lax.fori_loop(0, HELD // 4, mask_group, 0)

    def pick_faces(t, carry):
        fs_y[t] = pool[face_ref[t]].astype(BF16)
        return carry

    lax.fori_loop(0, 2 * FACE, pick_faces, 0)
    pl.semaphore_wait(barrier, n_gy + 1)

    def exchange(src, dst, send, recv, up, down):
        copies = [
            pltpu.make_async_remote_copy(
                src_ref=src.at[pl.ds(FACE, FACE)], dst_ref=dst.at[pl.ds(0, FACE)],
                send_sem=send.at[0], recv_sem=recv.at[0], device_id=up, device_id_type=MESH),
            pltpu.make_async_remote_copy(
                src_ref=src.at[pl.ds(0, FACE)], dst_ref=dst.at[pl.ds(FACE, FACE)],
                send_sem=send.at[1], recv_sem=recv.at[1], device_id=down, device_id_type=MESH),
        ]
        for copy in copies:
            copy.start()
        return copies

    y_copies = exchange(fs_y, fr_y, ys, yr, (gx, up_y), (gx, down_y))
    pool[POOL - 1] = jnp.zeros((BS, BS, LANES), F32)
    for copy in y_copies:
        copy.wait_recv()
    low_y = jnp.where(gy > 0, 1.0, 0.0).astype(F32)
    high_y = jnp.where(gy < n_gy - 1, 1.0, 0.0).astype(F32)

    def take_y(t, carry):
        pool[HELD + t] = fr_y[t].astype(F32) * low_y
        pool[HELD + FACE + t] = fr_y[FACE + t].astype(F32) * high_y
        return carry

    lax.fori_loop(0, FACE, take_y, 0)

    def pick_relays(t, carry):
        fs_x[t] = pool[relay_ref[t]].astype(BF16)
        return carry

    lax.fori_loop(0, 2 * FACE, pick_relays, 0)
    x_copies = exchange(fs_x, fr_x, xs, xr, (up_x, gy), (down_x, gy))
    build_bands(w_ref, bands)
    for copy in x_copies:
        copy.wait_recv()
    low_x = jnp.where(gx > 0, 1.0, 0.0).astype(F32)
    high_x = jnp.where(gx < n_gx - 1, 1.0, 0.0).astype(F32)

    def take_x(t, carry):
        pool[HELD + 2 * FACE + t] = fr_x[t].astype(F32) * low_x
        pool[HELD + 3 * FACE + t] = fr_x[FACE + t].astype(F32) * high_x
        return carry

    lax.fori_loop(0, FACE, take_x, 0)

    my_x, my_z, my_core = gy // 8, lax.rem(gy // 2, 4), lax.rem(gy, 2)

    def peer(g, i, sign):
        dz, dc = i // 2, i % 2
        dx = lax.rem(g + dz, 4)
        x = lax.rem(my_x + sign * dx + 4, 4)
        z = lax.rem(my_z + sign * dz + 4, 4)
        return 8 * x + 2 * z + lax.rem(my_core + dc, 2)

    half = 2 * C
    low_half = iota((BS, half), 1) < C
    first_row = iota((BS, half), 0) == 0
    last_row = iota((BS, half), 0) == BS - 1
    bias = jnp.concatenate([bias_ref[...], bias_ref[...]], axis=1)

    def block_rows(slot, ox, x):
        views = []
        for oy in range(3):
            around = [nbr_ref[slot, 9 * ox + 3 * oy + oz] for oz in range(3)]
            parts = [pool[around[0], x, :, 3 * half : 4 * half]]
            parts += [pool[around[1], x, :, t * half : (t + 1) * half] for t in range(4)]
            parts += [pool[around[2], x, :, 0:half]]
            views.append([jnp.where(low_half, parts[t + 1], parts[t]) for t in range(5)])
        before, here, after = views
        return (
            [jnp.where(last_row, b, h) for b, h in zip(before, here)],
            here,
            [jnp.where(first_row, a, h) for a, h in zip(after, here)],
        )

    def batch(g, carry):
        slots = [jnp.maximum(send_ref[peer(g, i, 1)], 0) for i in range(BATCH)]

        def assemble(pair, inner):
            two = [jnp.maximum(send_ref[peer_pair(g, pair, i)], 0) for i in range(2)]
            for xx in range(BS + 2):
                ox = 0 if xx == 0 else (2 if xx == BS + 1 else 1)
                x = (xx - 1) % BS
                first, second = block_rows(two[0], ox, x), block_rows(two[1], ox, x)
                for d in range(3):
                    for t in range(5):
                        joined = jnp.concatenate([first[d][t], second[d][t]], axis=0)
                        tiles[d, xx % 2, xx // 2, pl.ds(pl.multiple_of(16 * pair, 16), 16), t * half : (t + 1) * half] = (
                            joined.astype(BF16)
                        )
            return inner

        def peer_pair(g, pair, i):
            dx = lax.rem(g + pair, 4)
            x = lax.rem(my_x + dx, 4)
            z = lax.rem(my_z + pair, 4)
            return 8 * x + 2 * z + lax.rem(my_core + i, 2)

        lax.fori_loop(0, BATCH // 2, assemble, 0)

        def columns(q, inner):
            lanes = pl.ds(pl.multiple_of(half * q, half), 2 * half)
            sums = []
            for d in range(3):
                window = jnp.concatenate(
                    [
                        tiles[d, j % 2, j // 2 : j // 2 + 4, :, lanes].reshape(4 * BATCH * BS, 2 * half)
                        for j in range(4)
                    ],
                    axis=1,
                )
                product = jnp.dot(window, bands[d], preferred_element_type=F32)
                sums.append(product.reshape(4 * BATCH, BS, 4 * C))
            total = sums[1] + pltpu.roll(sums[0], 1, axis=1) + pltpu.roll(sums[2], BS - 1, axis=1)
            at = pl.ds(pl.multiple_of(half * q, half), half)
            for p in range(4):
                for b in range(BATCH):
                    for xo in range(2):
                        part = total[p * BATCH + b, :, xo * half : (xo + 1) * half] + bias
                        part = part * mask[slots[b], 2 * p + xo, :, at]
                        outbox[BATCH * g + b, 2 * p + xo, :, at] = part.astype(BF16)
            return inner

        lax.fori_loop(0, 4, columns, 0)

        for i in range(BATCH):
            def send(i=i):
                move(g, i).start()

            if i == 0:
                pl.when(g > 0)(send)
            else:
                send()
        return carry

    def move(g, i):
        k = BATCH * g + i
        return pltpu.make_async_remote_copy(
            src_ref=outbox.at[k], dst_ref=inbox.at[gy], send_sem=ss.at[k], recv_sem=rs.at[k],
            device_id=(gx, peer(g, i, 1)), device_id_type=MESH)

    def arrival(g, i):
        k = BATCH * g + i
        source = peer(g, i, -1)
        return pltpu.make_async_remote_copy(
            src_ref=outbox.at[k], dst_ref=inbox.at[source], send_sem=ss.at[k], recv_sem=rs.at[k],
            device_id=(gx, source), device_id_type=MESH)

    lax.fori_loop(0, HELD // BATCH, batch, 0)
    inbox[gy] = outbox[0]
    for copy in y_copies + x_copies:
        copy.wait_send()

    def collect(g, carry):
        for i in range(BATCH):
            def wait(i=i):
                move(g, i).wait_send()
                arrival(g, i).wait_recv()

            if i == 0:
                pl.when(g > 0)(wait)
            else:
                wait()
        return carry

    lax.fori_loop(0, HELD // BATCH, collect, 0)

    def place(r, carry):
        out_ref[r] = inbox[order_ref[r]]
        return carry

    lax.fori_loop(0, OUT, place, 0)


def on_device(features, occupancy, neighbors, face_lists, face_relays, send_slots, receive_order, weights, channel_bias):
    block = (BS, BS, LANES)
    smem = pl.BlockSpec(memory_space=pltpu.SMEM)
    vmem = pl.BlockSpec(memory_space=pltpu.VMEM)
    out = pl.pallas_call(
        kernel,
        out_shape=jax.ShapeDtypeStruct((OUT,) + block, BF16),
        in_specs=[smem] * 5 + [vmem, pl.BlockSpec(memory_space=pl.ANY), vmem, vmem],
        out_specs=vmem,
        scratch_shapes=[
            pltpu.VMEM((HELD,) + block, BF16),
            pltpu.VMEM((POOL,) + block, F32),
            pltpu.VMEM((HELD,) + block, F32),
            pltpu.VMEM((HELD, LANES), F32),
            pltpu.VMEM((3, 2, 5, BATCH * BS, LANES + 2 * C), BF16),
            pltpu.VMEM((3, 16 * C, 4 * C), BF16),
            pltpu.VMEM((HELD,) + block, BF16),
            pltpu.VMEM((HELD,) + block, BF16),
            pltpu.VMEM((2 * FACE,) + block, BF16),
            pltpu.VMEM((2 * FACE,) + block, BF16),
            pltpu.VMEM((2 * FACE,) + block, BF16),
            pltpu.VMEM((2 * FACE,) + block, BF16),
            pltpu.SemaphoreType.DMA((4,)),
            pltpu.SemaphoreType.DMA((2,)),
            pltpu.SemaphoreType.DMA((2,)),
            pltpu.SemaphoreType.DMA((2,)),
            pltpu.SemaphoreType.DMA((2,)),
            pltpu.SemaphoreType.DMA((HELD,)),
            pltpu.SemaphoreType.DMA((HELD,)),
        ],
        compiler_params=pltpu.CompilerParams(
            collective_id=0, has_side_effects=True, vmem_limit_bytes=48 << 20
        ),
    )(
        face_lists[0, 0],
        face_relays[0, 0],
        send_slots[0, 0, :, 0],
        receive_order[0, 0],
        neighbors[0, 0],
        occupancy[0, 0],
        features[0, 0],
        weights,
        channel_bias.reshape(1, C),
    )
    return out[None, None]


def solution(mesh):
    in_specs = (
        P("gx", "gy", None, None, None, None),
        P("gx", "gy", None, None),
        P("gx", "gy", None, None),
        P("gx", "gy", None),
        P("gx", "gy", None),
        P("gx", "gy", None, None),
        P("gx", "gy", None),
        P(),
        P(),
    )
    out_specs = P("gx", "gy", None, None, None, None)
    return jax.shard_map(
        on_device, mesh=mesh, in_specs=in_specs, out_specs=out_specs, check_vma=False
    )
```

profile of v0, /device:TPU:1, one launch (start us, length us, event | category | flops | bytes accessed | tf_op | source)
XLA Modules:
  0.0 62.4 jit_solution(14031453779694956438)
XLA Ops:
  0.0 0.8 %copy.11 = s32[1,1,32,25]{3,2,1,0:T(8,128)S(1)} copy(s32[1,1,32,25]{2,1,3,0:T(1,128)} %param.10) | data formatting | bytes 6400 | tf_op args[1]
  0.8 0.8 %copy.10 = s32[1,1,32,27]{3,2,1,0:T(8,128)S(1)} copy(s32[1,1,32,27]{2,1,3,0:T(1,128)} %param.11) | data formatting | bytes 6912 | tf_op args[2]
  1.6 0.0 copy-start
  1.6 1.6 %copy-done = bf16[1,1,32,8,8,512]{5,4,3,2,1,0:T(8,128)(2,1)S(1)} copy-done((bf16[1,1,32,8,8,512]{5,4,3,2,1,0:T(8,128)(2,1)S(1)}, bf16[1,1,32,8,8,512]{5,4,3,2,1,0:T(8,128)(2,1)}, u32[]{:S(2)}) %copy-start) | copy-done | bytes 2097176
  3.2 0.0 copy-start.1
  3.2 1.0 %copy-done.1 = bf16[27,64,64]{2,1,0:T(8,128)(2,1)S(1)} copy-done((bf16[27,64,64]{2,1,0:T(8,128)(2,1)S(1)}, bf16[27,64,64]{2,1,0:T(8,128)(2,1)}, u32[]{:S(2)}) %copy-start.1) | copy-done | bytes 221208
  4.2 0.0 copy-start.2
  4.2 0.7 %copy-done.2 = s32[1,1,8]{2,1,0:T(1,128)S(1)} copy-done((s32[1,1,8]{2,1,0:T(1,128)S(1)}, s32[1,1,8]{2,1,0:T(1,128)}, u32[]{:S(2)}) %copy-start.2) | copy-done | bytes 56
  4.8 0.0 copy-start.3
  4.8 0.7 %copy-done.3 = s32[1,1,8]{2,1,0:T(1,128)S(1)} copy-done((s32[1,1,8]{2,1,0:T(1,128)S(1)}, s32[1,1,8]{2,1,0:T(1,128)}, u32[]{:S(2)}) %copy-start.3) | copy-done | bytes 56
  5.5 0.0 copy-start.4
  5.5 0.7 %copy-done.4 = s32[1,1,32,1]{2,3,1,0:T(1,128)S(1)} copy-done((s32[1,1,32,1]{2,3,1,0:T(1,128)S(1)}, s32[1,1,32,1]{2,3,1,0:T(1,128)}, u32[]{:S(2)}) %copy-start.4) | copy-done | bytes 152
  6.1 0.0 copy-start.5
  6.1 0.7 %copy-done.5 = s32[1,1,16]{2,1,0:T(1,128)S(1)} copy-done((s32[1,1,16]{2,1,0:T(1,128)S(1)}, s32[1,1,16]{2,1,0:T(1,128)}, u32[]{:S(2)}) %copy-start.5) | copy-done | bytes 88
  6.8 0.0 copy-start.6
  6.8 0.7 %copy-done.6 = f32[64]{0:T(128)S(1)} copy-done((f32[64]{0:T(128)S(1)}, f32[64]{0:T(128)}, u32[]{:S(2)}) %copy-start.6) | copy-done | bytes 280
  7.5 53.9 %shard_map.91 = bf16[16,8,8,512]{3,2,1,0:T(8,128)(2,1)S(1)} custom-call(s32[8]{0:T(128)S(1)} %bitcast.13, s32[8]{0:T(128)S(1)} %bitcast.14, s32[32]{0:T(128)S(1)} %bitcast.15, s32[16]{0:T(128)S(1)} %bitcast.16, s32[32,27]{1,0:T(8,128)S(1)} %bitcast.12, s32[32,25]{1,0:T(8,128)S(1)} %bitcast.11, bf16[32,8,8,512]{3,2,1,0:T(8,128)(2,1)S(1)} %bitcast.10, ...), custom_call_target="tpu_custom_call" | custom-call | tf_op jit(solution)/shard_map/pallas_call | solution.py:293
  61.4 1.0 %copy.13 = bf16[1,1,16,8,8,512]{5,4,3,2,1,0:T(8,128)(2,1)} copy(bf16[1,1,16,8,8,512]{5,4,3,2,1,0:T(8,128)(2,1)S(1)} %bitcast.9) | data formatting | bytes 2097152
Async XLA Ops:
  1.6 1.6 %copy-start = (bf16[1,1,32,8,8,512]{5,4,3,2,1,0:T(8,128)(2,1)S(1)}, bf16[1,1,32,8,8,512]{5,4,3,2,1,0:T(8,128)(2,1)}, u32[]{:S(2)}) copy-start(bf16[1,1,32,8,8,512]{5,4,3,2,1,0:T(8,128)(2,1)} %param.9) | copy-start | bytes 6291460
  3.2 1.0 %copy-start.1 = (bf16[27,64,64]{2,1,0:T(8,128)(2,1)S(1)}, bf16[27,64,64]{2,1,0:T(8,128)(2,1)}, u32[]{:S(2)}) copy-start(bf16[27,64,64]{2,1,0:T(8,128)(2,1)} %w_ref.1) | copy-start | bytes 663556
  4.2 0.7 %copy-start.2 = (s32[1,1,8]{2,1,0:T(1,128)S(1)}, s32[1,1,8]{2,1,0:T(1,128)}, u32[]{:S(2)}) copy-start(s32[1,1,8]{2,1,0:T(1,128)} %param.12) | copy-start | bytes 100
  4.8 0.7 %copy-start.3 = (s32[1,1,8]{2,1,0:T(1,128)S(1)}, s32[1,1,8]{2,1,0:T(1,128)}, u32[]{:S(2)}) copy-start(s32[1,1,8]{2,1,0:T(1,128)} %param.13) | copy-start | bytes 100
  5.5 0.7 %copy-start.4 = (s32[1,1,32,1]{2,3,1,0:T(1,128)S(1)}, s32[1,1,32,1]{2,3,1,0:T(1,128)}, u32[]{:S(2)}) copy-start(s32[1,1,32,1]{2,3,1,0:T(1,128)} %param.14) | copy-start | bytes 388
  6.1 0.7 %copy-start.5 = (s32[1,1,16]{2,1,0:T(1,128)S(1)}, s32[1,1,16]{2,1,0:T(1,128)}, u32[]{:S(2)}) copy-start(s32[1,1,16]{2,1,0:T(1,128)} %param.15) | copy-start | bytes 196
  6.8 0.7 %copy-start.6 = (f32[64]{0:T(128)S(1)}, f32[64]{0:T(128)}, u32[]{:S(2)}) copy-start(f32[64]{0:T(128)} %param.17) | copy-start | bytes 772
where the time goes:
time: 62.9 us; the launch traced here: 62.4 us
  Pallas kernels  53.9 us (86%)
  local copies, waits for them, and re-layouts  8.42 us (13%)
    pallas_call x1, Pallas kernels, on_device(): pl.pallas_call(kernel, out_shape=jax.ShapeDtypeStruct((OUT,) + block, BF1...  53.9 us
    unnamed x17, local copies, waits for them, and re-layouts  8.42 us

commit v1 on v0

--- a/solution.py
+++ b/solution.py
@@ -24,14 +24,15 @@
 
 
 def occupancy_bits(words):
-    slots, width = words.shape
+    width, slots = words.shape
     voxels = BS**3
-    chunks = jnp.concatenate([words & 127, (words >> 7) & 127, words >> 14], axis=0)
+    chunks = jnp.concatenate([words & 127, (words >> 7) & 127, words >> 14], axis=1)
     voxel = iota((width, voxels), 1)
     pick = ((voxel * 3121) >> 16) == iota((width, voxels), 0)
-    picked = jnp.dot(
+    picked = lax.dot_general(
         chunks.astype(F32).astype(BF16),
         jnp.where(pick, 1.0, 0.0).astype(BF16),
+        (((0,), (0,)), ((), ())),
         preferred_element_type=F32,
     ).astype(jnp.int32)
     v = iota((slots, voxels), 1)
@@ -59,10 +60,10 @@
 
 
 def kernel(
-    face_ref, relay_ref, send_ref, order_ref, nbr_ref, occ_ref, feat_ref, w_ref, bias_ref,
+    face_hbm, relay_hbm, send_hbm, order_hbm, nbr_hbm, occ_hbm, feat_ref, w_hbm, bias_hbm,
     out_ref,
-    raw, pool, mask, bits, tiles, bands, outbox, inbox, fs_y, fr_y, fs_x, fr_x,
-    raw_sem, ys, yr, xs, xr, ss, rs,
+    face_ref, relay_ref, send_ref, order_ref, nbr_ref, occ_ref, w_ref, bias_ref, raw, pool, mask, bits, tiles, bands, outbox, inbox, fs_y, fr_y, fs_x, fr_x,
+    small_sem, raw_sem, ys, yr, xs, xr, ss, rs,
 ):
     gx = lax.axis_index("gx")
     gy = lax.axis_index("gy")
@@ -81,13 +82,24 @@
     for other in (up_x, down_x):
         pl.semaphore_signal(barrier, inc=1, device_id=(other, gy), device_id_type=MESH)
 
+    small = []
+    for i, (src, dst) in enumerate(
+        (
+            (occ_hbm, occ_ref), (face_hbm, face_ref), (relay_hbm, relay_ref), (send_hbm, send_ref),
+            (order_hbm, order_ref), (nbr_hbm, nbr_ref), (w_hbm, w_ref), (bias_hbm, bias_ref),
+        )
+    ):
+        load = pltpu.make_async_copy(src, dst, small_sem.at[i])
+        load.start()
+        small.append(load)
     loads = []
     for g in range(4):
         load = pltpu.make_async_copy(feat_ref.at[pl.ds(8 * g, 8)], raw.at[pl.ds(8 * g, 8)], raw_sem.at[g])
         load.start()
         loads.append(load)
 
-    bits[...] = occupancy_bits(occ_ref[...])
+    small[0].wait()
+    bits[...] = occupancy_bits(occ_ref[...].reshape(occ_ref.shape[0], HELD))
     rows = BS * BS
     own_row = jnp.where((iota((rows, LANES), 1) >> 3) == iota((rows, LANES), 0), 1.0, 0.0)
     spread = jnp.where((iota((LANES, LANES), 0) & 7) == (iota((LANES, LANES), 1) >> 6), 1.0, 0.0).astype(BF16)
@@ -100,12 +112,12 @@
         pool[pl.ds(4 * g, 4)] = raw[pl.ds(4 * g, 4)].astype(F32) * wide
         return carry
 
-    for load in loads:
+    for load in loads + small[1:]:
         load.wait()
     lax.fori_loop(0, HELD // 4, mask_group, 0)
 
     def pick_faces(t, carry):
-        fs_y[t] = pool[face_ref[t]].astype(BF16)
+        fs_y[t] = pool[face_ref[0, t]].astype(BF16)
         return carry
 
     lax.fori_loop(0, 2 * FACE, pick_faces, 0)
@@ -139,7 +151,7 @@
     lax.fori_loop(0, FACE, take_y, 0)
 
     def pick_relays(t, carry):
-        fs_x[t] = pool[relay_ref[t]].astype(BF16)
+        fs_x[t] = pool[relay_ref[0, t]].astype(BF16)
         return carry
 
     lax.fori_loop(0, 2 * FACE, pick_relays, 0)
@@ -175,7 +187,7 @@
     def block_rows(slot, ox, x):
         views = []
         for oy in range(3):
-            around = [nbr_ref[slot, 9 * ox + 3 * oy + oz] for oz in range(3)]
+            around = [nbr_ref[9 * ox + 3 * oy + oz, 0, slot] for oz in range(3)]
             parts = [pool[around[0], x, :, 3 * half : 4 * half]]
             parts += [pool[around[1], x, :, t * half : (t + 1) * half] for t in range(4)]
             parts += [pool[around[2], x, :, 0:half]]
@@ -188,10 +200,10 @@
         )
 
     def batch(g, carry):
-        slots = [jnp.maximum(send_ref[peer(g, i, 1)], 0) for i in range(BATCH)]
+        slots = [jnp.maximum(send_ref[0, peer(g, i, 1)], 0) for i in range(BATCH)]
 
         def assemble(pair, inner):
-            two = [jnp.maximum(send_ref[peer_pair(g, pair, i)], 0) for i in range(2)]
+            two = [jnp.maximum(send_ref[0, peer_pair(g, pair, i)], 0) for i in range(2)]
             for xx in range(BS + 2):
                 ox = 0 if xx == 0 else (2 if xx == BS + 1 else 1)
                 x = (xx - 1) % BS
@@ -280,7 +292,7 @@
     lax.fori_loop(0, HELD // BATCH, collect, 0)
 
     def place(r, carry):
-        out_ref[r] = inbox[order_ref[r]]
+        out_ref[r] = inbox[order_ref[0, r]]
         return carry
 
     lax.fori_loop(0, OUT, place, 0)
@@ -288,14 +300,20 @@
 
 def on_device(features, occupancy, neighbors, face_lists, face_relays, send_slots, receive_order, weights, channel_bias):
     block = (BS, BS, LANES)
-    smem = pl.BlockSpec(memory_space=pltpu.SMEM)
-    vmem = pl.BlockSpec(memory_space=pltpu.VMEM)
     out = pl.pallas_call(
         kernel,
         out_shape=jax.ShapeDtypeStruct((OUT,) + block, BF16),
-        in_specs=[smem] * 5 + [vmem, pl.BlockSpec(memory_space=pl.ANY), vmem, vmem],
-        out_specs=vmem,
+        in_specs=[pl.BlockSpec(memory_space=pltpu.HBM)] * 9,
+        out_specs=pl.BlockSpec(memory_space=pltpu.VMEM),
         scratch_shapes=[
+            pltpu.SMEM((1, 2 * FACE), jnp.int32),
+            pltpu.SMEM((1, 2 * FACE), jnp.int32),
+            pltpu.SMEM((1, HELD), jnp.int32),
+            pltpu.SMEM((1, OUT), jnp.int32),
+            pltpu.SMEM((27, 1, HELD), jnp.int32),
+            pltpu.VMEM((occupancy.shape[-1], 1, HELD), jnp.int32),
+            pltpu.VMEM(weights.shape, BF16),
+            pltpu.VMEM((1, C), F32),
             pltpu.VMEM((HELD,) + block, BF16),
             pltpu.VMEM((POOL,) + block, F32),
             pltpu.VMEM((HELD,) + block, F32),
@@ -308,6 +326,7 @@
             pltpu.VMEM((2 * FACE,) + block, BF16),
             pltpu.VMEM((2 * FACE,) + block, BF16),
             pltpu.VMEM((2 * FACE,) + block, BF16),
+            pltpu.SemaphoreType.DMA((8,)),
             pltpu.SemaphoreType.DMA((4,)),
             pltpu.SemaphoreType.DMA((2,)),
             pltpu.SemaphoreType.DMA((2,)),
@@ -317,15 +336,15 @@
             pltpu.SemaphoreType.DMA((HELD,)),
         ],
         compiler_params=pltpu.CompilerParams(
-            collective_id=0, has_side_effects=True, vmem_limit_bytes=48 << 20
+            collective_id=0, has_side_effects=True, vmem_limit_bytes=60 << 20
         ),
     )(
-        face_lists[0, 0],
-        face_relays[0, 0],
-        send_slots[0, 0, :, 0],
-        receive_order[0, 0],
-        neighbors[0, 0],
-        occupancy[0, 0],
+        face_lists[0],
+        face_relays[0],
+        send_slots[0, :, :, 0],
+        receive_order[0],
+        jnp.transpose(neighbors[0], (2, 0, 1)),
+        jnp.transpose(occupancy[0], (2, 0, 1)),
         features[0, 0],
         weights,
         channel_bias.reshape(1, C),

time: 62.9 us -> 57.6 us (0.916)
  local copies, waits for them, and re-layouts: 8.42 us -> 2.29 us
  Pallas kernels: 53.9 us -> 55.2 us
    unnamed x17 -> x1, local copies, waits for them, and re-layouts: 8.42 us -> 2.29 us
    pallas_call x1, Pallas kernels: 53.9 us -> 55.2 us  [on_device(): pl.pallas_call(kernel, out_shape=jax.ShapeDtypeStruct((OUT,) + block, BF1...]
where the time goes in v1:
time: 57.6 us; the launch traced here: 57.5 us
  Pallas kernels  55.2 us (96%)
  local copies, waits for them, and re-layouts  2.29 us (4%)
    pallas_call x1, Pallas kernels, on_device(): pl.pallas_call(kernel, out_shape=jax.ShapeDtypeStruct((OUT,) + block, BF1...  55.2 us
    unnamed x1, local copies, waits for them, and re-layouts  2.29 us

profile of v1, /device:TPU:1, one launch (start us, length us, event | category | flops | bytes accessed | tf_op | source)
XLA Modules:
  0.0 57.5 jit_solution(12567740186911995609)
XLA Ops:
  0.0 55.2 %shard_map.91 = bf16[16,8,8,512]{3,2,1,0:T(8,128)(2,1)} custom-call(s32[1,8]{1,0:T(1,128)} %bitcast.17, s32[1,8]{1,0:T(1,128)} %bitcast.18, s32[1,32]{1,0:T(1,128)} %bitcast.19, s32[1,16]{1,0:T(1,128)} %bitcast.20, s32[27,1,32]{2,1,0:T(1,128)} %bitcast.15, s32[25,1,32]{2,1,0:T(1,128)} %bitcast.16, bf16[32,8,8,512]{3,2,1,0:T(8,128)(2,1)} %bitcast.14, ...), custom_call_target="tpu_custom_call" | custom-call | tf_op jit(solution)/shard_map/pallas_call | solution.py:303
  55.2 2.3 %copy.11 = bf16[1,1,16,8,8,512]{5,4,3,2,1,0:T(8,128)(2,1)} copy(bf16[1,1,16,8,8,512]{5,4,3,2,1,0:T(8,128)(2,1)} %bitcast.13) | data formatting | bytes 2097152

commit v2 on v1

--- a/solution.py
+++ b/solution.py
@@ -13,6 +13,9 @@
 OUT = 16
 POOL = 49
 BATCH = 8
+EARLY = 1
+INNER = 15
+SHELL = 20
 WORD_BITS = 21
 MESH = pl.DeviceIdType.MESH
 F32 = jnp.float32
@@ -43,15 +46,14 @@
     return ((chunk >> shift) & 1).astype(F32)
 
 
-def build_bands(w_ref, bands):
+def build_bands(w_ref, bands, z_order, swapped):
     zero = jnp.zeros((C, C), BF16)
     for d in range(3):
         for a in range(3):
             taps = [w_ref[9 * a + 3 * d + c] for c in range(3)]
-            for k, rz in enumerate((1, 0, 3, 2)):
-                left = taps[rz] if rz <= 2 else zero
-                right = taps[rz - 1] if rz >= 1 else zero
-                pair = jnp.concatenate([left, right], axis=1)
+            for k, rz in enumerate(z_order):
+                ends = [taps[rz] if rz <= 2 else zero, taps[rz - 1] if rz >= 1 else zero]
+                pair = jnp.concatenate(ends[::-1] if swapped else ends, axis=1)
                 for xo in range(2):
                     bands[d, pl.ds((a + xo) * 4 * C + k * C, C), xo * 2 * C : (xo + 1) * 2 * C] = pair
         blank = jnp.zeros((4 * C, 2 * C), BF16)
@@ -62,8 +64,10 @@
 def kernel(
     face_hbm, relay_hbm, send_hbm, order_hbm, nbr_hbm, occ_hbm, feat_ref, w_hbm, bias_hbm,
     out_ref,
-    face_ref, relay_ref, send_ref, order_ref, nbr_ref, occ_ref, w_ref, bias_ref, raw, pool, mask, bits, tiles, bands, outbox, inbox, fs_y, fr_y, fs_x, fr_x,
-    small_sem, raw_sem, ys, yr, xs, xr, ss, rs,
+    face_ref, relay_ref, send_ref, order_ref, nbr_ref, occ_ref, w_ref, bias_ref, raw, pool, mask, bits,
+    inner_tiles, inner_bands, tiles, bands, stage, inner_out, inner_in, shell_out, shell_in,
+    fs_y, fr_y, fs_x, fr_x,
+    small_sem, raw_sem, ys, yr, xs, xr, inner_ss, inner_rs, shell_ss, shell_rs,
 ):
     gx = lax.axis_index("gx")
     gy = lax.axis_index("gy")
@@ -112,7 +116,10 @@
         pool[pl.ds(4 * g, 4)] = raw[pl.ds(4 * g, 4)].astype(F32) * wide
         return carry
 
-    for load in loads + small[1:]:
+    for load in small[1:]:
+        load.wait()
+    build_bands(w_ref, inner_bands, (0, 1, 2, 3), True)
+    for load in loads:
         load.wait()
     lax.fori_loop(0, HELD // 4, mask_group, 0)
 
@@ -138,51 +145,111 @@
 
     y_copies = exchange(fs_y, fr_y, ys, yr, (gx, up_y), (gx, down_y))
     pool[POOL - 1] = jnp.zeros((BS, BS, LANES), F32)
-    for copy in y_copies:
-        copy.wait_recv()
-    low_y = jnp.where(gy > 0, 1.0, 0.0).astype(F32)
-    high_y = jnp.where(gy < n_gy - 1, 1.0, 0.0).astype(F32)
-
-    def take_y(t, carry):
-        pool[HELD + t] = fr_y[t].astype(F32) * low_y
-        pool[HELD + FACE + t] = fr_y[FACE + t].astype(F32) * high_y
-        return carry
-
-    lax.fori_loop(0, FACE, take_y, 0)
-
-    def pick_relays(t, carry):
-        fs_x[t] = pool[relay_ref[0, t]].astype(BF16)
-        return carry
-
-    lax.fori_loop(0, 2 * FACE, pick_relays, 0)
-    x_copies = exchange(fs_x, fr_x, xs, xr, (up_x, gy), (down_x, gy))
-    build_bands(w_ref, bands)
-    for copy in x_copies:
-        copy.wait_recv()
-    low_x = jnp.where(gx > 0, 1.0, 0.0).astype(F32)
-    high_x = jnp.where(gx < n_gx - 1, 1.0, 0.0).astype(F32)
-
-    def take_x(t, carry):
-        pool[HELD + 2 * FACE + t] = fr_x[t].astype(F32) * low_x
-        pool[HELD + 3 * FACE + t] = fr_x[FACE + t].astype(F32) * high_x
-        return carry
-
-    lax.fori_loop(0, FACE, take_x, 0)
 
     my_x, my_z, my_core = gy // 8, lax.rem(gy // 2, 4), lax.rem(gy, 2)
 
-    def peer(g, i, sign):
-        dz, dc = i // 2, i % 2
-        dx = lax.rem(g + dz, 4)
-        x = lax.rem(my_x + sign * dx + 4, 4)
+    def peer(g, dz, dc, sign):
+        x = lax.rem(my_x + sign * lax.rem(g + dz, 4) + 4, 4)
         z = lax.rem(my_z + sign * dz + 4, 4)
         return 8 * x + 2 * z + lax.rem(my_core + dc, 2)
 
     half = 2 * C
-    low_half = iota((BS, half), 1) < C
-    first_row = iota((BS, half), 0) == 0
-    last_row = iota((BS, half), 0) == BS - 1
+    lane = iota((BS, half), 1)
+    row = iota((BS, half), 0)
+    low_half = lane < C
+    first_row = row == 0
+    last_row = row == BS - 1
+    edge_row = first_row | last_row
     bias = jnp.concatenate([bias_ref[...], bias_ref[...]], axis=1)
+
+    def slot_of(g, dz, dc):
+        return jnp.maximum(send_ref[0, peer(g, dz, dc, 1)], 0)
+
+    def turn(v, by):
+        return pltpu.roll(v, by % BS, axis=0)
+
+    def product(source, weight, planes, lanes):
+        sums = []
+        for d in range(3):
+            window = jnp.concatenate(
+                [
+                    source(d, j % 2, j // 2, lanes).reshape(planes * BATCH * BS, 2 * half)
+                    for j in range(4)
+                ],
+                axis=1,
+            )
+            part = jnp.dot(window, weight[d], preferred_element_type=F32)
+            sums.append(part.reshape(planes * BATCH, BS, 4 * C))
+        return sums[1] + pltpu.roll(sums[0], 1, axis=1) + pltpu.roll(sums[2], BS - 1, axis=1)
+
+    def mover(out, into, send, recv):
+        def outgoing(g, i):
+            k = BATCH * g + i
+            return pltpu.make_async_remote_copy(
+                src_ref=out.at[k], dst_ref=into.at[gy], send_sem=send.at[k], recv_sem=recv.at[k],
+                device_id=(gx, peer(g, i // 2, i % 2, 1)), device_id_type=MESH)
+
+        def incoming(g, i):
+            k = BATCH * g + i
+            source = peer(g, i // 2, i % 2, -1)
+            return pltpu.make_async_remote_copy(
+                src_ref=out.at[k], dst_ref=into.at[source], send_sem=send.at[k], recv_sem=recv.at[k],
+                device_id=(gx, source), device_id_type=MESH)
+
+        def each(g, act):
+            for i in range(BATCH):
+                if i == 0:
+                    pl.when(g > 0)(lambda: act(g, 0))
+                else:
+                    act(g, i)
+
+        def start(g):
+            each(g, lambda g, i: outgoing(g, i).start())
+
+        def finish(g, carry):
+            def wait(g, i):
+                outgoing(g, i).wait_send()
+                incoming(g, i).wait_recv()
+
+            each(g, wait)
+            return carry
+
+        return start, finish
+
+    start_inner, finish_inner = mover(inner_out, inner_in, inner_ss, inner_rs)
+    start_shell, finish_shell = mover(shell_out, shell_in, shell_ss, shell_rs)
+
+    def inner_batch(g, carry):
+        def gather(pair, inner):
+            two = [slot_of(g, pair, dc) for dc in range(2)]
+            for x in range(BS):
+                joined = jnp.concatenate([pool[two[0], x], pool[two[1], x]], axis=0)
+                inner_tiles[x % 2, x // 2, pl.ds(pl.multiple_of(2 * BS * pair, 2 * BS), 2 * BS), :] = joined.astype(BF16)
+            return inner
+
+        lax.fori_loop(0, BATCH // 2, gather, 0)
+        slots = [slot_of(g, i // 2, i % 2) for i in range(BATCH)]
+
+        def columns(q, inner):
+            lanes = pl.ds(pl.multiple_of(half * q, half), 2 * half)
+            total = product(
+                lambda d, odd, first, lanes: inner_tiles[odd, first : first + 3, :, lanes], inner_bands, 3, lanes)
+            here = pl.ds(pl.multiple_of(half * q, half), half)
+            above = pl.ds(pl.multiple_of(half * q + half, half), half)
+            for b in range(BATCH):
+                parts = []
+                for x in range(6):
+                    keep = jnp.where(low_half, mask[slots[b], x + 1, :, above], mask[slots[b], x + 1, :, here])
+                    at = (x % 2) * half
+                    parts.append((total[(x // 2) * BATCH + b, :, at : at + half] + bias) * keep)
+                packed = [jnp.where(edge_row, turn(parts[3], 6 - 2 * m), parts[m]) for m in range(3)]
+                for m, part in enumerate(packed + parts[4:]):
+                    inner_out[BATCH * g + b, 5 * q + m] = part.astype(BF16)
+            return inner
+
+        lax.fori_loop(0, 3, columns, 0)
+        start_inner(g)
+        return carry
 
     def block_rows(slot, ox, x):
         views = []
@@ -199,11 +266,9 @@
             [jnp.where(first_row, a, h) for a, h in zip(after, here)],
         )
 
-    def batch(g, carry):
-        slots = [jnp.maximum(send_ref[0, peer(g, i, 1)], 0) for i in range(BATCH)]
-
+    def shell_batch(g, carry):
         def assemble(pair, inner):
-            two = [jnp.maximum(send_ref[0, peer_pair(g, pair, i)], 0) for i in range(2)]
+            two = [slot_of(g, pair, dc) for dc in range(2)]
             for xx in range(BS + 2):
                 ox = 0 if xx == 0 else (2 if xx == BS + 1 else 1)
                 x = (xx - 1) % BS
@@ -211,88 +276,107 @@
                 for d in range(3):
                     for t in range(5):
                         joined = jnp.concatenate([first[d][t], second[d][t]], axis=0)
-                        tiles[d, xx % 2, xx // 2, pl.ds(pl.multiple_of(16 * pair, 16), 16), t * half : (t + 1) * half] = (
-                            joined.astype(BF16)
-                        )
+                        tiles[
+                            d, xx % 2, xx // 2, pl.ds(pl.multiple_of(2 * BS * pair, 2 * BS), 2 * BS), t * half : (t + 1) * half
+                        ] = joined.astype(BF16)
             return inner
 
-        def peer_pair(g, pair, i):
-            dx = lax.rem(g + pair, 4)
-            x = lax.rem(my_x + dx, 4)
-            z = lax.rem(my_z + pair, 4)
-            return 8 * x + 2 * z + lax.rem(my_core + i, 2)
-
         lax.fori_loop(0, BATCH // 2, assemble, 0)
+        slots = [slot_of(g, i // 2, i % 2) for i in range(BATCH)]
 
         def columns(q, inner):
             lanes = pl.ds(pl.multiple_of(half * q, half), 2 * half)
-            sums = []
-            for d in range(3):
-                window = jnp.concatenate(
-                    [
-                        tiles[d, j % 2, j // 2 : j // 2 + 4, :, lanes].reshape(4 * BATCH * BS, 2 * half)
-                        for j in range(4)
-                    ],
-                    axis=1,
-                )
-                product = jnp.dot(window, bands[d], preferred_element_type=F32)
-                sums.append(product.reshape(4 * BATCH, BS, 4 * C))
-            total = sums[1] + pltpu.roll(sums[0], 1, axis=1) + pltpu.roll(sums[2], BS - 1, axis=1)
-            at = pl.ds(pl.multiple_of(half * q, half), half)
-            for p in range(4):
-                for b in range(BATCH):
-                    for xo in range(2):
-                        part = total[p * BATCH + b, :, xo * half : (xo + 1) * half] + bias
-                        part = part * mask[slots[b], 2 * p + xo, :, at]
-                        outbox[BATCH * g + b, 2 * p + xo, :, at] = part.astype(BF16)
+            total = product(lambda d, odd, first, lanes: tiles[d, odd, first : first + 4, :, lanes], bands, 4, lanes)
+            here = pl.ds(pl.multiple_of(half * q, half), half)
+            for b in range(BATCH):
+                for x in range(BS):
+                    at = (x % 2) * half
+                    part = total[(x // 2) * BATCH + b, :, at : at + half] + bias
+                    stage[b, x, :, here] = part * mask[slots[b], x, :, here]
             return inner
 
         lax.fori_loop(0, 4, columns, 0)
 
-        for i in range(BATCH):
-            def send(i=i):
-                move(g, i).start()
-
-            if i == 0:
-                pl.when(g > 0)(send)
-            else:
-                send()
-        return carry
-
-    def move(g, i):
-        k = BATCH * g + i
-        return pltpu.make_async_remote_copy(
-            src_ref=outbox.at[k], dst_ref=inbox.at[gy], send_sem=ss.at[k], recv_sem=rs.at[k],
-            device_id=(gx, peer(g, i, 1)), device_id_type=MESH)
-
-    def arrival(g, i):
-        k = BATCH * g + i
-        source = peer(g, i, -1)
-        return pltpu.make_async_remote_copy(
-            src_ref=outbox.at[k], dst_ref=inbox.at[source], send_sem=ss.at[k], recv_sem=rs.at[k],
-            device_id=(gx, source), device_id_type=MESH)
-
-    lax.fori_loop(0, HELD // BATCH, batch, 0)
-    inbox[gy] = outbox[0]
+        def pack(b, inner):
+            k = BATCH * g + b
+            for side, x in enumerate((0, BS - 1)):
+                for t in range(4):
+                    shell_out[k, 4 * side + t] = stage[b, x, :, t * half : (t + 1) * half].astype(BF16)
+            for x in range(6):
+                parts = [stage[b, x + 1, :, t * half : (t + 1) * half] for t in range(4)]
+                shell_out[k, 8 + x] = jnp.where(low_half, parts[0], parts[3]).astype(BF16)
+                packed = parts[0]
+                for t in range(1, 4):
+                    packed = jnp.where((row == 2 * t) | (row == 2 * t - 1), turn(parts[t], 2 * t), packed)
+                shell_out[k, 14 + x] = packed.astype(BF16)
+            return inner
+
+        lax.fori_loop(0, BATCH, pack, 0)
+        start_shell(g)
+        return carry
+
+    lax.fori_loop(0, EARLY, inner_batch, 0)
+    for copy in y_copies:
+        copy.wait_recv()
+    low_y = jnp.where(gy > 0, 1.0, 0.0).astype(F32)
+    high_y = jnp.where(gy < n_gy - 1, 1.0, 0.0).astype(F32)
+
+    def take_y(t, carry):
+        pool[HELD + t] = fr_y[t].astype(F32) * low_y
+        pool[HELD + FACE + t] = fr_y[FACE + t].astype(F32) * high_y
+        return carry
+
+    lax.fori_loop(0, FACE, take_y, 0)
+
+    def pick_relays(t, carry):
+        fs_x[t] = pool[relay_ref[0, t]].astype(BF16)
+        return carry
+
+    lax.fori_loop(0, 2 * FACE, pick_relays, 0)
+    x_copies = exchange(fs_x, fr_x, xs, xr, (up_x, gy), (down_x, gy))
+    lax.fori_loop(EARLY, HELD // BATCH, inner_batch, 0)
+    build_bands(w_ref, bands, (1, 0, 3, 2), False)
+    for copy in x_copies:
+        copy.wait_recv()
+    low_x = jnp.where(gx > 0, 1.0, 0.0).astype(F32)
+    high_x = jnp.where(gx < n_gx - 1, 1.0, 0.0).astype(F32)
+
+    def take_x(t, carry):
+        pool[HELD + 2 * FACE + t] = fr_x[t].astype(F32) * low_x
+        pool[HELD + 3 * FACE + t] = fr_x[FACE + t].astype(F32) * high_x
+        return carry
+
+    lax.fori_loop(0, FACE, take_x, 0)
+    lax.fori_loop(0, HELD // BATCH, shell_batch, 0)
+    inner_in[gy] = inner_out[0]
+    shell_in[gy] = shell_out[0]
     for copy in y_copies + x_copies:
         copy.wait_send()
-
-    def collect(g, carry):
-        for i in range(BATCH):
-            def wait(i=i):
-                move(g, i).wait_send()
-                arrival(g, i).wait_recv()
-
-            if i == 0:
-                pl.when(g > 0)(wait)
-            else:
-                wait()
-        return carry
-
-    lax.fori_loop(0, HELD // BATCH, collect, 0)
+    lax.fori_loop(0, HELD // BATCH, finish_inner, 0)
+    lax.fori_loop(0, HELD // BATCH, finish_shell, 0)
 
     def place(r, carry):
-        out_ref[r] = inbox[order_ref[0, r]]
+        source = order_ref[0, r]
+        for side, x in enumerate((0, BS - 1)):
+            for t in range(4):
+                out_ref[r, x, :, t * half : (t + 1) * half] = shell_in[source, 4 * side + t]
+        arrived = [[inner_in[source, 5 * q + m].astype(F32) for m in range(5)] for q in range(3)]
+        for x in range(6):
+            middle = []
+            for q in range(3):
+                if x == 3:
+                    first, second, third = arrived[q][:3]
+                    middle.append(
+                        jnp.where(row <= 2, turn(first, 2), jnp.where(row <= 4, turn(second, 4), turn(third, 6))))
+                else:
+                    middle.append(arrived[q][x if x < 3 else x - 1])
+            ends = shell_in[source, 8 + x].astype(F32)
+            packed = shell_in[source, 14 + x].astype(F32)
+            chain = [ends] + middle + [ends]
+            for t in range(4):
+                inner = jnp.where(low_half, chain[t], chain[t + 1])
+                whole = jnp.where(edge_row, turn(packed, -2 * t), inner)
+                out_ref[r, x + 1, :, t * half : (t + 1) * half] = whole.astype(BF16)
         return carry
 
     lax.fori_loop(0, OUT, place, 0)
@@ -318,10 +402,15 @@
             pltpu.VMEM((POOL,) + block, F32),
             pltpu.VMEM((HELD,) + block, F32),
             pltpu.VMEM((HELD, LANES), F32),
+            pltpu.VMEM((2, 4, BATCH * BS, LANES), BF16),
+            pltpu.VMEM((3, 16 * C, 4 * C), BF16),
             pltpu.VMEM((3, 2, 5, BATCH * BS, LANES + 2 * C), BF16),
             pltpu.VMEM((3, 16 * C, 4 * C), BF16),
-            pltpu.VMEM((HELD,) + block, BF16),
-            pltpu.VMEM((HELD,) + block, BF16),
+            pltpu.VMEM((BATCH,) + block, F32),
+            pltpu.VMEM((HELD, INNER, BS, 2 * C), BF16),
+            pltpu.VMEM((HELD, INNER, BS, 2 * C), BF16),
+            pltpu.VMEM((HELD, SHELL, BS, 2 * C), BF16),
+            pltpu.VMEM((HELD, SHELL, BS, 2 * C), BF16),
             pltpu.VMEM((2 * FACE,) + block, BF16),
             pltpu.VMEM((2 * FACE,) + block, BF16),
             pltpu.VMEM((2 * FACE,) + block, BF16),
@@ -332,6 +421,8 @@
             pltpu.SemaphoreType.DMA((2,)),
             pltpu.SemaphoreType.DMA((2,)),
             pltpu.SemaphoreType.DMA((2,)),
+            pltpu.SemaphoreType.DMA((HELD,)),
+            pltpu.SemaphoreType.DMA((HELD,)),
             pltpu.SemaphoreType.DMA((HELD,)),
             pltpu.SemaphoreType.DMA((HELD,)),
         ],

time: 57.6 us -> 51.4 us (0.89)
  Pallas kernels: 55.2 us -> 48.9 us
    pallas_call x1, Pallas kernels: 55.2 us -> 48.9 us  [on_device(): pl.pallas_call(kernel, out_shape=jax.ShapeDtypeStruct((OUT,) + block, BF1...]
where the time goes in v2:
time: 51.4 us; the launch traced here: 51.2 us
  Pallas kernels  48.9 us (95%)
  local copies, waits for them, and re-layouts  2.29 us (4%)
    pallas_call x1, Pallas kernels, on_device(): pl.pallas_call(kernel, out_shape=jax.ShapeDtypeStruct((OUT,) + block, BF1...  48.9 us
    unnamed x1, local copies, waits for them, and re-layouts  2.29 us

profile of v2, /device:TPU:1, one launch (start us, length us, event | category | flops | bytes accessed | tf_op | source)
XLA Modules:
  0.0 51.2 jit_solution(7685666423052859769)
XLA Ops:
  0.0 48.9 %shard_map.91 = bf16[16,8,8,512]{3,2,1,0:T(8,128)(2,1)} custom-call(s32[1,8]{1,0:T(1,128)} %bitcast.17, s32[1,8]{1,0:T(1,128)} %bitcast.18, s32[1,32]{1,0:T(1,128)} %bitcast.19, s32[1,16]{1,0:T(1,128)} %bitcast.20, s32[27,1,32]{2,1,0:T(1,128)} %bitcast.15, s32[25,1,32]{2,1,0:T(1,128)} %bitcast.16, bf16[32,8,8,512]{3,2,1,0:T(8,128)(2,1)} %bitcast.14, ...), custom_call_target="tpu_custom_call" | custom-call | tf_op jit(solution)/shard_map/pallas_call | solution.py:387
  48.9 2.3 %copy.11 = bf16[1,1,16,8,8,512]{5,4,3,2,1,0:T(8,128)(2,1)} copy(bf16[1,1,16,8,8,512]{5,4,3,2,1,0:T(8,128)(2,1)} %bitcast.13) | data formatting | bytes 2097152

commit v3 on v2

--- a/solution.py
+++ b/solution.py
@@ -14,6 +14,7 @@
 POOL = 49
 BATCH = 8
 EARLY = 1
+GROUP = 4
 INNER = 15
 SHELL = 20
 WORD_BITS = 21
@@ -64,7 +65,7 @@
 def kernel(
     face_hbm, relay_hbm, send_hbm, order_hbm, nbr_hbm, occ_hbm, feat_ref, w_hbm, bias_hbm,
     out_ref,
-    face_ref, relay_ref, send_ref, order_ref, nbr_ref, occ_ref, w_ref, bias_ref, raw, pool, mask, bits,
+    face_ref, relay_ref, send_ref, order_ref, nbr_ref, occ_ref, w_ref, bias_ref, chosen, raw, pool, mask, bits,
     inner_tiles, inner_bands, tiles, bands, stage, inner_out, inner_in, shell_out, shell_in,
     fs_y, fr_y, fs_x, fr_x,
     small_sem, raw_sem, ys, yr, xs, xr, inner_ss, inner_rs, shell_ss, shell_rs,
@@ -123,8 +124,44 @@
         load.wait()
     lax.fori_loop(0, HELD // 4, mask_group, 0)
 
+    half = 2 * C
+    lane = iota((BS, half), 1)
+    row = iota((BS, half), 0)
+    low_half = lane < C
+    first_row = row == 0
+    last_row = row == BS - 1
+    edge_row = first_row | last_row
+
+    def turn(v, by):
+        return pltpu.roll(v, by % BS, axis=0)
+
+    def pack_shell(source, block, into, k):
+        for side, x in enumerate((0, BS - 1)):
+            for t in range(4):
+                into[k, 4 * side + t] = source[block, x, :, t * half : (t + 1) * half].astype(BF16)
+        for x in range(6):
+            parts = [source[block, x + 1, :, t * half : (t + 1) * half] for t in range(4)]
+            into[k, 8 + x] = jnp.where(low_half, parts[0], parts[3]).astype(BF16)
+            packed = parts[0]
+            for t in range(1, 4):
+                packed = jnp.where((row == 2 * t) | (row == 2 * t - 1), turn(parts[t], 2 * t), packed)
+            into[k, 14 + x] = packed.astype(BF16)
+
+    def unpack_shell(source, k, block, factor):
+        for side, x in enumerate((0, BS - 1)):
+            for t in range(4):
+                pool[block, x, :, t * half : (t + 1) * half] = source[k, 4 * side + t].astype(F32) * factor
+        for x in range(6):
+            ends = source[k, 8 + x].astype(F32) * factor
+            packed = source[k, 14 + x].astype(F32) * factor
+            for t in range(4):
+                whole = turn(packed, -2 * t)
+                if t in (0, 3):
+                    whole = jnp.where(edge_row, whole, ends)
+                pool[block, x + 1, :, t * half : (t + 1) * half] = whole
+
     def pick_faces(t, carry):
-        fs_y[t] = pool[face_ref[0, t]].astype(BF16)
+        pack_shell(pool, face_ref[0, t], fs_y, t)
         return carry
 
     lax.fori_loop(0, 2 * FACE, pick_faces, 0)
@@ -148,39 +185,50 @@
 
     my_x, my_z, my_core = gy // 8, lax.rem(gy // 2, 4), lax.rem(gy, 2)
 
-    def peer(g, dz, dc, sign):
-        x = lax.rem(my_x + sign * lax.rem(g + dz, 4) + 4, 4)
+    offsets = (
+        ((2, 1), (2, 3), (1, 2), (3, 2)),
+        ((1, 1), (3, 3), (1, 3), (3, 1)),
+        ((1, 0), (3, 0), (0, 1), (0, 3)),
+        ((2, 0), (0, 2), (2, 2), (0, 0)),
+    )
+    x_codes = [sum(offsets[g][i][0] * 4**g for g in range(4)) for i in range(4)]
+    z_codes = [sum(offsets[g][i][1] * 4**g for g in range(4)) for i in range(4)]
+
+    def peer(g, i, dc, sign):
+        power = lax.shift_left(1, 2 * g)
+        dx = lax.rem(x_codes[i] // power, 4)
+        dz = lax.rem(z_codes[i] // power, 4)
+        x = lax.rem(my_x + sign * dx + 4, 4)
         z = lax.rem(my_z + sign * dz + 4, 4)
         return 8 * x + 2 * z + lax.rem(my_core + dc, 2)
 
-    half = 2 * C
-    lane = iota((BS, half), 1)
-    row = iota((BS, half), 0)
-    low_half = lane < C
-    first_row = row == 0
-    last_row = row == BS - 1
-    edge_row = first_row | last_row
     bias = jnp.concatenate([bias_ref[...], bias_ref[...]], axis=1)
 
-    def slot_of(g, dz, dc):
-        return jnp.maximum(send_ref[0, peer(g, dz, dc, 1)], 0)
-
-    def turn(v, by):
-        return pltpu.roll(v, by % BS, axis=0)
-
-    def product(source, weight, planes, lanes):
+    def slot_of(g, i, dc):
+        return jnp.maximum(send_ref[0, peer(g, i, dc, 1)], 0)
+
+    def product(source, weight, planes, groups):
         sums = []
         for d in range(3):
             window = jnp.concatenate(
                 [
-                    source(d, j % 2, j // 2, lanes).reshape(planes * BATCH * BS, 2 * half)
-                    for j in range(4)
+                    jnp.concatenate(
+                        [
+                            source(d, j % 2, j // 2, lanes).reshape(planes * BATCH * BS, 2 * half)
+                            for j in range(4)
+                        ],
+                        axis=1,
+                    )
+                    for lanes in groups
                 ],
-                axis=1,
+                axis=0,
             )
             part = jnp.dot(window, weight[d], preferred_element_type=F32)
-            sums.append(part.reshape(planes * BATCH, BS, 4 * C))
+            sums.append(part.reshape(len(groups) * planes * BATCH, BS, 4 * C))
         return sums[1] + pltpu.roll(sums[0], 1, axis=1) + pltpu.roll(sums[2], BS - 1, axis=1)
+
+    def at_lanes(tile, count):
+        return pl.ds(pl.multiple_of(half * tile, half), count * half)
 
     def mover(out, into, send, recv):
         def outgoing(g, i):
@@ -198,8 +246,8 @@
 
         def each(g, act):
             for i in range(BATCH):
-                if i == 0:
-                    pl.when(g > 0)(lambda: act(g, 0))
+                if i == BATCH - 2:
+                    pl.when(g < HELD // BATCH - 1)(lambda: act(g, BATCH - 2))
                 else:
                     act(g, i)
 
@@ -216,26 +264,31 @@
 
         return start, finish
 
+    def choose(g, carry):
+        for i in range(BATCH):
+            chosen[BATCH * g + i] = slot_of(g, i // 2, i % 2)
+        return carry
+
+    lax.fori_loop(0, HELD // BATCH, choose, 0)
     start_inner, finish_inner = mover(inner_out, inner_in, inner_ss, inner_rs)
     start_shell, finish_shell = mover(shell_out, shell_in, shell_ss, shell_rs)
 
     def inner_batch(g, carry):
         def gather(pair, inner):
-            two = [slot_of(g, pair, dc) for dc in range(2)]
+            two = [chosen[BATCH * g + 2 * pair + dc] for dc in range(2)]
             for x in range(BS):
                 joined = jnp.concatenate([pool[two[0], x], pool[two[1], x]], axis=0)
                 inner_tiles[x % 2, x // 2, pl.ds(pl.multiple_of(2 * BS * pair, 2 * BS), 2 * BS), :] = joined.astype(BF16)
             return inner
 
         lax.fori_loop(0, BATCH // 2, gather, 0)
-        slots = [slot_of(g, i // 2, i % 2) for i in range(BATCH)]
+        slots = [chosen[BATCH * g + i] for i in range(BATCH)]
 
         def columns(q, inner):
-            lanes = pl.ds(pl.multiple_of(half * q, half), 2 * half)
             total = product(
-                lambda d, odd, first, lanes: inner_tiles[odd, first : first + 3, :, lanes], inner_bands, 3, lanes)
-            here = pl.ds(pl.multiple_of(half * q, half), half)
-            above = pl.ds(pl.multiple_of(half * q + half, half), half)
+                lambda d, odd, first, lanes: inner_tiles[odd, first : first + 3, :, lanes],
+                inner_bands, 3, [at_lanes(q, 2)])
+            here, above = at_lanes(q, 1), at_lanes(q + 1, 1)
             for b in range(BATCH):
                 parts = []
                 for x in range(6):
@@ -268,7 +321,7 @@
 
     def shell_batch(g, carry):
         def assemble(pair, inner):
-            two = [slot_of(g, pair, dc) for dc in range(2)]
+            two = [chosen[BATCH * g + 2 * pair + dc] for dc in range(2)]
             for xx in range(BS + 2):
                 ox = 0 if xx == 0 else (2 if xx == BS + 1 else 1)
                 x = (xx - 1) % BS
@@ -282,33 +335,25 @@
             return inner
 
         lax.fori_loop(0, BATCH // 2, assemble, 0)
-        slots = [slot_of(g, i // 2, i % 2) for i in range(BATCH)]
-
-        def columns(q, inner):
-            lanes = pl.ds(pl.multiple_of(half * q, half), 2 * half)
-            total = product(lambda d, odd, first, lanes: tiles[d, odd, first : first + 4, :, lanes], bands, 4, lanes)
-            here = pl.ds(pl.multiple_of(half * q, half), half)
-            for b in range(BATCH):
-                for x in range(BS):
-                    at = (x % 2) * half
-                    part = total[(x // 2) * BATCH + b, :, at : at + half] + bias
-                    stage[b, x, :, here] = part * mask[slots[b], x, :, here]
+        slots = [chosen[BATCH * g + i] for i in range(BATCH)]
+
+        def columns(step, inner):
+            total = product(
+                lambda d, odd, first, lanes: tiles[d, odd, first : first + 4, :, lanes],
+                bands, 4, [at_lanes(GROUP * step + i, 2) for i in range(GROUP)])
+            for i in range(GROUP):
+                here = at_lanes(GROUP * step + i, 1)
+                for b in range(BATCH):
+                    for x in range(BS):
+                        at = (x % 2) * half
+                        part = total[(4 * i + x // 2) * BATCH + b, :, at : at + half] + bias
+                        stage[b, x, :, here] = part * mask[slots[b], x, :, here]
             return inner
 
-        lax.fori_loop(0, 4, columns, 0)
+        lax.fori_loop(0, 4 // GROUP, columns, 0)
 
         def pack(b, inner):
-            k = BATCH * g + b
-            for side, x in enumerate((0, BS - 1)):
-                for t in range(4):
-                    shell_out[k, 4 * side + t] = stage[b, x, :, t * half : (t + 1) * half].astype(BF16)
-            for x in range(6):
-                parts = [stage[b, x + 1, :, t * half : (t + 1) * half] for t in range(4)]
-                shell_out[k, 8 + x] = jnp.where(low_half, parts[0], parts[3]).astype(BF16)
-                packed = parts[0]
-                for t in range(1, 4):
-                    packed = jnp.where((row == 2 * t) | (row == 2 * t - 1), turn(parts[t], 2 * t), packed)
-                shell_out[k, 14 + x] = packed.astype(BF16)
+            pack_shell(stage, b, shell_out, BATCH * g + b)
             return inner
 
         lax.fori_loop(0, BATCH, pack, 0)
@@ -322,14 +367,14 @@
     high_y = jnp.where(gy < n_gy - 1, 1.0, 0.0).astype(F32)
 
     def take_y(t, carry):
-        pool[HELD + t] = fr_y[t].astype(F32) * low_y
-        pool[HELD + FACE + t] = fr_y[FACE + t].astype(F32) * high_y
+        unpack_shell(fr_y, t, HELD + t, low_y)
+        unpack_shell(fr_y, FACE + t, HELD + FACE + t, high_y)
         return carry
 
     lax.fori_loop(0, FACE, take_y, 0)
 
     def pick_relays(t, carry):
-        fs_x[t] = pool[relay_ref[0, t]].astype(BF16)
+        pack_shell(pool, relay_ref[0, t], fs_x, t)
         return carry
 
     lax.fori_loop(0, 2 * FACE, pick_relays, 0)
@@ -342,14 +387,14 @@
     high_x = jnp.where(gx < n_gx - 1, 1.0, 0.0).astype(F32)
 
     def take_x(t, carry):
-        pool[HELD + 2 * FACE + t] = fr_x[t].astype(F32) * low_x
-        pool[HELD + 3 * FACE + t] = fr_x[FACE + t].astype(F32) * high_x
+        unpack_shell(fr_x, t, HELD + 2 * FACE + t, low_x)
+        unpack_shell(fr_x, FACE + t, HELD + 3 * FACE + t, high_x)
         return carry
 
     lax.fori_loop(0, FACE, take_x, 0)
     lax.fori_loop(0, HELD // BATCH, shell_batch, 0)
-    inner_in[gy] = inner_out[0]
-    shell_in[gy] = shell_out[0]
+    inner_in[gy] = inner_out[HELD - 2]
+    shell_in[gy] = shell_out[HELD - 2]
     for copy in y_copies + x_copies:
         copy.wait_send()
     lax.fori_loop(0, HELD // BATCH, finish_inner, 0)
@@ -398,6 +443,7 @@
             pltpu.VMEM((occupancy.shape[-1], 1, HELD), jnp.int32),
             pltpu.VMEM(weights.shape, BF16),
             pltpu.VMEM((1, C), F32),
+            pltpu.SMEM((HELD,), jnp.int32),
             pltpu.VMEM((HELD,) + block, BF16),
             pltpu.VMEM((POOL,) + block, F32),
             pltpu.VMEM((HELD,) + block, F32),
@@ -411,10 +457,10 @@
             pltpu.VMEM((HELD, INNER, BS, 2 * C), BF16),
             pltpu.VMEM((HELD, SHELL, BS, 2 * C), BF16),
             pltpu.VMEM((HELD, SHELL, BS, 2 * C), BF16),
-            pltpu.VMEM((2 * FACE,) + block, BF16),
-            pltpu.VMEM((2 * FACE,) + block, BF16),
-            pltpu.VMEM((2 * FACE,) + block, BF16),
-            pltpu.VMEM((2 * FACE,) + block, BF16),
+            pltpu.VMEM((2 * FACE, SHELL, BS, 2 * C), BF16),
+            pltpu.VMEM((2 * FACE, SHELL, BS, 2 * C), BF16),
+            pltpu.VMEM((2 * FACE, SHELL, BS, 2 * C), BF16),
+            pltpu.VMEM((2 * FACE, SHELL, BS, 2 * C), BF16),
             pltpu.SemaphoreType.DMA((8,)),
             pltpu.SemaphoreType.DMA((4,)),
             pltpu.SemaphoreType.DMA((2,)),

time: 51.4 us -> 47 us (0.914); the launches traced: 51.2 us -> 46.1 us
  Pallas kernels: 48.9 us -> 43.9 us
    pallas_call x1, Pallas kernels: 48.9 us -> 43.9 us  [on_device(): pl.pallas_call(kernel, out_shape=jax.ShapeDtypeStruct((OUT,) + block, BF1...]
where the time goes in v3:
time: 47 us; the launch traced here: 46.1 us
  Pallas kernels  43.9 us (93%)
  local copies, waits for them, and re-layouts  2.29 us (5%)
    pallas_call x1, Pallas kernels, on_device(): pl.pallas_call(kernel, out_shape=jax.ShapeDtypeStruct((OUT,) + block, BF1...  43.9 us
    unnamed x1, local copies, waits for them, and re-layouts  2.29 us

profile of v3, /device:TPU:1, one launch (start us, length us, event | category | flops | bytes accessed | tf_op | source)
XLA Modules:
  0.0 46.1 jit_solution(11341221928222380231)
XLA Ops:
  0.0 43.9 %shard_map.91 = bf16[16,8,8,512]{3,2,1,0:T(8,128)(2,1)} custom-call(s32[1,8]{1,0:T(1,128)} %bitcast.17, s32[1,8]{1,0:T(1,128)} %bitcast.18, s32[1,32]{1,0:T(1,128)} %bitcast.19, s32[1,16]{1,0:T(1,128)} %bitcast.20, s32[27,1,32]{2,1,0:T(1,128)} %bitcast.15, s32[25,1,32]{2,1,0:T(1,128)} %bitcast.16, bf16[32,8,8,512]{3,2,1,0:T(8,128)(2,1)} %bitcast.14, ...), custom_call_target="tpu_custom_call" | custom-call | tf_op jit(solution)/shard_map/pallas_call | solution.py:432
  43.9 2.3 %copy.11 = bf16[1,1,16,8,8,512]{5,4,3,2,1,0:T(8,128)(2,1)} copy(bf16[1,1,16,8,8,512]{5,4,3,2,1,0:T(8,128)(2,1)} %bitcast.13) | data formatting | bytes 2097152

commit v4 on v3

--- a/solution.py
+++ b/solution.py
@@ -15,8 +15,8 @@
 BATCH = 8
 EARLY = 1
 GROUP = 4
-INNER = 15
-SHELL = 20
+INNER = 14
+SHELL = 19
 WORD_BITS = 21
 MESH = pl.DeviceIdType.MESH
 F32 = jnp.float32
@@ -135,30 +135,41 @@
     def turn(v, by):
         return pltpu.roll(v, by % BS, axis=0)
 
+    def between(parts):
+        return [jnp.where(low_half, parts[q + 1], parts[q]) for q in range(3)]
+
+    def joined(ends, middle):
+        chain = [ends] + middle + [ends]
+        return [jnp.where(low_half, chain[t], chain[t + 1]) for t in range(4)]
+
     def pack_shell(source, block, into, k):
         for side, x in enumerate((0, BS - 1)):
             for t in range(4):
                 into[k, 4 * side + t] = source[block, x, :, t * half : (t + 1) * half].astype(BF16)
+        strips = []
         for x in range(6):
             parts = [source[block, x + 1, :, t * half : (t + 1) * half] for t in range(4)]
             into[k, 8 + x] = jnp.where(low_half, parts[0], parts[3]).astype(BF16)
-            packed = parts[0]
-            for t in range(1, 4):
-                packed = jnp.where((row == 2 * t) | (row == 2 * t - 1), turn(parts[t], 2 * t), packed)
-            into[k, 14 + x] = packed.astype(BF16)
+            strips += between(parts)
+        for m in range(5):
+            packed = strips[4 * m]
+            for t, strip in enumerate(strips[4 * m + 1 : 4 * m + 4], 1):
+                packed = jnp.where((row == 2 * t) | (row == 2 * t - 1), turn(strip, 2 * t), packed)
+            into[k, 14 + m] = packed.astype(BF16)
+
+    def outer_y(source, k):
+        packed = [source[k, 14 + m].astype(F32) for m in range(5)]
+        return [turn(packed[i // 4], -2 * (i % 4)) for i in range(18)]
 
     def unpack_shell(source, k, block, factor):
         for side, x in enumerate((0, BS - 1)):
             for t in range(4):
                 pool[block, x, :, t * half : (t + 1) * half] = source[k, 4 * side + t].astype(F32) * factor
+        strips = outer_y(source, k)
         for x in range(6):
-            ends = source[k, 8 + x].astype(F32) * factor
-            packed = source[k, 14 + x].astype(F32) * factor
-            for t in range(4):
-                whole = turn(packed, -2 * t)
-                if t in (0, 3):
-                    whole = jnp.where(edge_row, whole, ends)
-                pool[block, x + 1, :, t * half : (t + 1) * half] = whole
+            ends = source[k, 8 + x].astype(F32)
+            for t, tile in enumerate(joined(ends, strips[3 * x : 3 * x + 3])):
+                pool[block, x + 1, :, t * half : (t + 1) * half] = tile * factor
 
     def pick_faces(t, carry):
         pack_shell(pool, face_ref[0, t], fs_y, t)
@@ -277,30 +288,30 @@
         def gather(pair, inner):
             two = [chosen[BATCH * g + 2 * pair + dc] for dc in range(2)]
             for x in range(BS):
-                joined = jnp.concatenate([pool[two[0], x], pool[two[1], x]], axis=0)
-                inner_tiles[x % 2, x // 2, pl.ds(pl.multiple_of(2 * BS * pair, 2 * BS), 2 * BS), :] = joined.astype(BF16)
+                both = jnp.concatenate([pool[two[0], x], pool[two[1], x]], axis=0)
+                inner_tiles[x % 2, x // 2, pl.ds(pl.multiple_of(2 * BS * pair, 2 * BS), 2 * BS), :] = both.astype(BF16)
             return inner
 
         lax.fori_loop(0, BATCH // 2, gather, 0)
         slots = [chosen[BATCH * g + i] for i in range(BATCH)]
 
-        def columns(q, inner):
-            total = product(
-                lambda d, odd, first, lanes: inner_tiles[odd, first : first + 3, :, lanes],
-                inner_bands, 3, [at_lanes(q, 2)])
-            here, above = at_lanes(q, 1), at_lanes(q + 1, 1)
-            for b in range(BATCH):
-                parts = []
-                for x in range(6):
-                    keep = jnp.where(low_half, mask[slots[b], x + 1, :, above], mask[slots[b], x + 1, :, here])
-                    at = (x % 2) * half
-                    parts.append((total[(x // 2) * BATCH + b, :, at : at + half] + bias) * keep)
-                packed = [jnp.where(edge_row, turn(parts[3], 6 - 2 * m), parts[m]) for m in range(3)]
-                for m, part in enumerate(packed + parts[4:]):
-                    inner_out[BATCH * g + b, 5 * q + m] = part.astype(BF16)
-            return inner
-
-        lax.fori_loop(0, 3, columns, 0)
+        total = product(
+            lambda d, odd, first, lanes: inner_tiles[odd, first : first + 3, :, lanes],
+            inner_bands, 3, [pl.ds(half * q, 2 * half) for q in range(3)])
+        for b in range(BATCH):
+            parts = []
+            for x in range(6):
+                keep = between([mask[slots[b], x + 1, :, t * half : (t + 1) * half] for t in range(4)])
+                at = (x % 2) * half
+                for q in range(3):
+                    value = total[(3 * q + x // 2) * BATCH + b, :, at : at + half]
+                    parts.append((value + bias) * keep[q])
+            packed = []
+            for m in range(4):
+                for j in range(3):
+                    packed.append(jnp.where(edge_row, turn(parts[4 * m + 3], 6 - 2 * j), parts[4 * m + j]))
+            for m, part in enumerate(packed + parts[16:]):
+                inner_out[BATCH * g + b, m] = part.astype(BF16)
         start_inner(g)
         return carry
 
@@ -328,10 +339,10 @@
                 first, second = block_rows(two[0], ox, x), block_rows(two[1], ox, x)
                 for d in range(3):
                     for t in range(5):
-                        joined = jnp.concatenate([first[d][t], second[d][t]], axis=0)
+                        both = jnp.concatenate([first[d][t], second[d][t]], axis=0)
                         tiles[
                             d, xx % 2, xx // 2, pl.ds(pl.multiple_of(2 * BS * pair, 2 * BS), 2 * BS), t * half : (t + 1) * half
-                        ] = joined.astype(BF16)
+                        ] = both.astype(BF16)
             return inner
 
         lax.fori_loop(0, BATCH // 2, assemble, 0)
@@ -405,23 +416,22 @@
         for side, x in enumerate((0, BS - 1)):
             for t in range(4):
                 out_ref[r, x, :, t * half : (t + 1) * half] = shell_in[source, 4 * side + t]
-        arrived = [[inner_in[source, 5 * q + m].astype(F32) for m in range(5)] for q in range(3)]
+        arrived = [inner_in[source, m].astype(F32) for m in range(INNER)]
+        strips = outer_y(shell_in, source)
+        middle = []
+        for i in range(18):
+            if i >= 16:
+                tile = arrived[i - 4]
+            elif i % 4 < 3:
+                tile = arrived[3 * (i // 4) + i % 4]
+            else:
+                first, second, third = arrived[3 * (i // 4) : 3 * (i // 4) + 3]
+                tile = jnp.where(row <= 2, turn(first, 2), jnp.where(row <= 4, turn(second, 4), turn(third, 6)))
+            middle.append(jnp.where(edge_row, strips[i], tile))
         for x in range(6):
-            middle = []
-            for q in range(3):
-                if x == 3:
-                    first, second, third = arrived[q][:3]
-                    middle.append(
-                        jnp.where(row <= 2, turn(first, 2), jnp.where(row <= 4, turn(second, 4), turn(third, 6))))
-                else:
-                    middle.append(arrived[q][x if x < 3 else x - 1])
             ends = shell_in[source, 8 + x].astype(F32)
-            packed = shell_in[source, 14 + x].astype(F32)
-            chain = [ends] + middle + [ends]
-            for t in range(4):
-                inner = jnp.where(low_half, chain[t], chain[t + 1])
-                whole = jnp.where(edge_row, turn(packed, -2 * t), inner)
-                out_ref[r, x + 1, :, t * half : (t + 1) * half] = whole.astype(BF16)
+            for t, tile in enumerate(joined(ends, middle[3 * x : 3 * x + 3])):
+                out_ref[r, x + 1, :, t * half : (t + 1) * half] = tile.astype(BF16)
         return carry
 
     lax.fori_loop(0, OUT, place, 0)
@@ -473,18 +483,23 @@
             pltpu.SemaphoreType.DMA((HELD,)),
         ],
         compiler_params=pltpu.CompilerParams(
-            collective_id=0, has_side_effects=True, vmem_limit_bytes=60 << 20
+            collective_id=0, has_side_effects=True, vmem_limit_bytes=50 << 20
         ),
     )(
-        face_lists[0],
-        face_relays[0],
-        send_slots[0, :, :, 0],
-        receive_order[0],
-        jnp.transpose(neighbors[0], (2, 0, 1)),
-        jnp.transpose(occupancy[0], (2, 0, 1)),
-        features[0, 0],
-        weights,
-        channel_bias.reshape(1, C),
+        *(
+            pltpu.with_memory_space_constraint(operand, pltpu.HBM)
+            for operand in (
+                face_lists[0],
+                face_relays[0],
+                send_slots[0, :, :, 0],
+                receive_order[0],
+                jnp.transpose(neighbors[0], (2, 0, 1)),
+                jnp.transpose(occupancy[0], (2, 0, 1)),
+                features[0, 0],
+                weights,
+                channel_bias.reshape(1, C),
+            )
+        )
     )
     return out[None, None]
 

time: 47 us -> 42.9 us (0.913); the launches traced: 46.1 us -> 42.8 us
  Pallas kernels: 43.9 us -> 41.8 us
  local copies, waits for them, and re-layouts: 2.29 us -> 0.97 us
    pallas_call x1, Pallas kernels: 43.9 us -> 41.8 us  [on_device(): pl.pallas_call(kernel, out_shape=jax.ShapeDtypeStruct((OUT,) + block, BF1...]
    unnamed x1, local copies, waits for them, and re-layouts: 2.29 us -> 0.97 us
where the time goes in v4:
time: 42.9 us; the launch traced here: 42.8 us
  Pallas kernels  41.8 us (97%)
  local copies, waits for them, and re-layouts  0.97 us (2%)
    pallas_call x1, Pallas kernels, on_device(): pl.pallas_call(kernel, out_shape=jax.ShapeDtypeStruct((OUT,) + block, BF1...  41.8 us
    unnamed x1, local copies, waits for them, and re-layouts  0.97 us

profile of v4, /device:TPU:1, one launch (start us, length us, event | category | flops | bytes accessed | tf_op | source)
XLA Modules:
  0.0 42.8 jit_solution(10155040997462504969)
XLA Ops:
  0.0 41.8 %shard_map.91 = bf16[16,8,8,512]{3,2,1,0:T(8,128)(2,1)S(1)} custom-call(s32[1,8]{1,0:T(1,128)} %bitcast.17, s32[1,8]{1,0:T(1,128)} %bitcast.18, s32[1,32]{1,0:T(1,128)} %bitcast.19, s32[1,16]{1,0:T(1,128)} %bitcast.20, s32[27,1,32]{2,1,0:T(1,128)} %bitcast.15, s32[25,1,32]{2,1,0:T(1,128)} %bitcast.16, bf16[32,8,8,512]{3,2,1,0:T(8,128)(2,1)} %bitcast.14, ...), custom_call_target="tpu_custom_call" | custom-call | tf_op jit(solution)/shard_map/pallas_call | solution.py:442
  41.8 1.0 %copy.11 = bf16[1,1,16,8,8,512]{5,4,3,2,1,0:T(8,128)(2,1)} copy(bf16[1,1,16,8,8,512]{5,4,3,2,1,0:T(8,128)(2,1)S(1)} %bitcast.13) | data formatting | bytes 2097152

commit v5 on v4

--- a/solution.py
+++ b/solution.py
@@ -12,8 +12,8 @@
 FACE = 4
 OUT = 16
 POOL = 49
-BATCH = 8
-EARLY = 1
+BATCH = 4
+EARLY = 2
 GROUP = 4
 INNER = 14
 SHELL = 19
@@ -171,39 +171,55 @@
             for t, tile in enumerate(joined(ends, strips[3 * x : 3 * x + 3])):
                 pool[block, x + 1, :, t * half : (t + 1) * half] = tile * factor
 
-    def pick_faces(t, carry):
-        pack_shell(pool, face_ref[0, t], fs_y, t)
-        return carry
-
-    lax.fori_loop(0, 2 * FACE, pick_faces, 0)
     pl.semaphore_wait(barrier, n_gy + 1)
 
-    def exchange(src, dst, send, recv, up, down):
-        copies = [
-            pltpu.make_async_remote_copy(
-                src_ref=src.at[pl.ds(FACE, FACE)], dst_ref=dst.at[pl.ds(0, FACE)],
-                send_sem=send.at[0], recv_sem=recv.at[0], device_id=up, device_id_type=MESH),
-            pltpu.make_async_remote_copy(
-                src_ref=src.at[pl.ds(0, FACE)], dst_ref=dst.at[pl.ds(FACE, FACE)],
-                send_sem=send.at[1], recv_sem=recv.at[1], device_id=down, device_id_type=MESH),
-        ]
-        for copy in copies:
-            copy.start()
-        return copies
-
-    y_copies = exchange(fs_y, fr_y, ys, yr, (gx, up_y), (gx, down_y))
+    def exchange(out, into, send, recv, up, down, index, first, low, high):
+        def copy(t, device):
+            slot = lax.rem(t + FACE, 2 * FACE)
+            return pltpu.make_async_remote_copy(
+                src_ref=out.at[t], dst_ref=into.at[slot], send_sem=send.at[t], recv_sem=recv.at[slot],
+                device_id=device, device_id_type=MESH)
+
+        def pick(t, carry):
+            pack_shell(pool, index[0, t], out, t)
+            copy(t, down).start()
+            pack_shell(pool, index[0, FACE + t], out, FACE + t)
+            copy(FACE + t, up).start()
+            return carry
+
+        def take(t, carry):
+            copy(FACE + t, up).wait_recv()
+            unpack_shell(into, t, first + t, low)
+            copy(t, down).wait_recv()
+            unpack_shell(into, FACE + t, first + FACE + t, high)
+            return carry
+
+        def settle(t, carry):
+            copy(t, down).wait_send()
+            copy(FACE + t, up).wait_send()
+            return carry
+
+        return [lambda act=act: lax.fori_loop(0, FACE, act, 0) for act in (pick, take, settle)]
+
+    def inside(condition):
+        return jnp.where(condition, 1.0, 0.0).astype(F32)
+
+    send_y, take_y, settle_y = exchange(
+        fs_y, fr_y, ys, yr, (gx, up_y), (gx, down_y), face_ref, HELD, inside(gy > 0), inside(gy < n_gy - 1))
+    send_x, take_x, settle_x = exchange(
+        fs_x, fr_x, xs, xr, (up_x, gy), (down_x, gy), relay_ref, HELD + 2 * FACE,
+        inside(gx > 0), inside(gx < n_gx - 1))
+    send_y()
     pool[POOL - 1] = jnp.zeros((BS, BS, LANES), F32)
 
     my_x, my_z, my_core = gy // 8, lax.rem(gy // 2, 4), lax.rem(gy, 2)
 
     offsets = (
-        ((2, 1), (2, 3), (1, 2), (3, 2)),
-        ((1, 1), (3, 3), (1, 3), (3, 1)),
-        ((1, 0), (3, 0), (0, 1), (0, 3)),
-        ((2, 0), (0, 2), (2, 2), (0, 0)),
+        ((2, 1), (1, 2)), ((2, 3), (3, 2)), ((1, 1), (3, 3)), ((1, 3), (3, 1)),
+        ((1, 0), (3, 0)), ((0, 1), (0, 3)), ((2, 0), (0, 2)), ((2, 2), (0, 0)),
     )
-    x_codes = [sum(offsets[g][i][0] * 4**g for g in range(4)) for i in range(4)]
-    z_codes = [sum(offsets[g][i][1] * 4**g for g in range(4)) for i in range(4)]
+    x_codes = [sum(pair[i][0] * 4**g for g, pair in enumerate(offsets)) for i in range(2)]
+    z_codes = [sum(pair[i][1] * 4**g for g, pair in enumerate(offsets)) for i in range(2)]
 
     def peer(g, i, dc, sign):
         power = lax.shift_left(1, 2 * g)
@@ -372,42 +388,16 @@
         return carry
 
     lax.fori_loop(0, EARLY, inner_batch, 0)
-    for copy in y_copies:
-        copy.wait_recv()
-    low_y = jnp.where(gy > 0, 1.0, 0.0).astype(F32)
-    high_y = jnp.where(gy < n_gy - 1, 1.0, 0.0).astype(F32)
-
-    def take_y(t, carry):
-        unpack_shell(fr_y, t, HELD + t, low_y)
-        unpack_shell(fr_y, FACE + t, HELD + FACE + t, high_y)
-        return carry
-
-    lax.fori_loop(0, FACE, take_y, 0)
-
-    def pick_relays(t, carry):
-        pack_shell(pool, relay_ref[0, t], fs_x, t)
-        return carry
-
-    lax.fori_loop(0, 2 * FACE, pick_relays, 0)
-    x_copies = exchange(fs_x, fr_x, xs, xr, (up_x, gy), (down_x, gy))
+    take_y()
+    send_x()
     lax.fori_loop(EARLY, HELD // BATCH, inner_batch, 0)
     build_bands(w_ref, bands, (1, 0, 3, 2), False)
-    for copy in x_copies:
-        copy.wait_recv()
-    low_x = jnp.where(gx > 0, 1.0, 0.0).astype(F32)
-    high_x = jnp.where(gx < n_gx - 1, 1.0, 0.0).astype(F32)
-
-    def take_x(t, carry):
-        unpack_shell(fr_x, t, HELD + 2 * FACE + t, low_x)
-        unpack_shell(fr_x, FACE + t, HELD + 3 * FACE + t, high_x)
-        return carry
-
-    lax.fori_loop(0, FACE, take_x, 0)
+    take_x()
     lax.fori_loop(0, HELD // BATCH, shell_batch, 0)
     inner_in[gy] = inner_out[HELD - 2]
     shell_in[gy] = shell_out[HELD - 2]
-    for copy in y_copies + x_copies:
-        copy.wait_send()
+    settle_y()
+    settle_x()
     lax.fori_loop(0, HELD // BATCH, finish_inner, 0)
     lax.fori_loop(0, HELD // BATCH, finish_shell, 0)
 
@@ -473,10 +463,10 @@
             pltpu.VMEM((2 * FACE, SHELL, BS, 2 * C), BF16),
             pltpu.SemaphoreType.DMA((8,)),
             pltpu.SemaphoreType.DMA((4,)),
-            pltpu.SemaphoreType.DMA((2,)),
-            pltpu.SemaphoreType.DMA((2,)),
-            pltpu.SemaphoreType.DMA((2,)),
-            pltpu.SemaphoreType.DMA((2,)),
+            pltpu.SemaphoreType.DMA((2 * FACE,)),
+            pltpu.SemaphoreType.DMA((2 * FACE,)),
+            pltpu.SemaphoreType.DMA((2 * FACE,)),
+            pltpu.SemaphoreType.DMA((2 * FACE,)),
             pltpu.SemaphoreType.DMA((HELD,)),
             pltpu.SemaphoreType.DMA((HELD,)),
             pltpu.SemaphoreType.DMA((HELD,)),

time: 42.9 us -> 40.8 us (0.951)
  Pallas kernels: 41.8 us -> 39.7 us
    pallas_call x1, Pallas kernels: 41.8 us -> 39.7 us  [on_device(): pl.pallas_call(kernel, out_shape=jax.ShapeDtypeStruct((OUT,) + block, BF1...]
where the time goes in v5:
time: 40.8 us; the launch traced here: 40.6 us
  Pallas kernels  39.7 us (97%)
  local copies, waits for them, and re-layouts  0.97 us (2%)
    pallas_call x1, Pallas kernels, on_device(): pl.pallas_call(kernel, out_shape=jax.ShapeDtypeStruct((OUT,) + block, BF1...  39.7 us
    unnamed x1, local copies, waits for them, and re-layouts  0.97 us

profile of v5, /device:TPU:1, one launch (start us, length us, event | category | flops | bytes accessed | tf_op | source)
XLA Modules:
  0.0 40.6 jit_solution(8261225558628291607)
XLA Ops:
  0.0 39.7 %shard_map.91 = bf16[16,8,8,512]{3,2,1,0:T(8,128)(2,1)S(1)} custom-call(s32[1,8]{1,0:T(1,128)} %bitcast.17, s32[1,8]{1,0:T(1,128)} %bitcast.18, s32[1,32]{1,0:T(1,128)} %bitcast.19, s32[1,16]{1,0:T(1,128)} %bitcast.20, s32[27,1,32]{2,1,0:T(1,128)} %bitcast.15, s32[25,1,32]{2,1,0:T(1,128)} %bitcast.16, bf16[32,8,8,512]{3,2,1,0:T(8,128)(2,1)} %bitcast.14, ...), custom_call_target="tpu_custom_call" | custom-call | tf_op jit(solution)/shard_map/pallas_call | solution.py:432
  39.7 1.0 %copy.11 = bf16[1,1,16,8,8,512]{5,4,3,2,1,0:T(8,128)(2,1)} copy(bf16[1,1,16,8,8,512]{5,4,3,2,1,0:T(8,128)(2,1)S(1)} %bitcast.13) | data formatting | bytes 2097152

commit v6 on v5

--- a/solution.py
+++ b/solution.py
@@ -120,9 +120,9 @@
     for load in small[1:]:
         load.wait()
     build_bands(w_ref, inner_bands, (0, 1, 2, 3), True)
-    for load in loads:
+    for g, load in enumerate(loads):
         load.wait()
-    lax.fori_loop(0, HELD // 4, mask_group, 0)
+        lax.fori_loop(2 * g, 2 * g + 2, mask_group, 0)
 
     half = 2 * C
     lane = iota((BS, half), 1)
@@ -215,8 +215,8 @@
     my_x, my_z, my_core = gy // 8, lax.rem(gy // 2, 4), lax.rem(gy, 2)
 
     offsets = (
-        ((2, 1), (1, 2)), ((2, 3), (3, 2)), ((1, 1), (3, 3)), ((1, 3), (3, 1)),
-        ((1, 0), (3, 0)), ((0, 1), (0, 3)), ((2, 0), (0, 2)), ((2, 2), (0, 0)),
+        ((2, 1), (1, 2)), ((2, 3), (3, 2)), ((2, 0), (0, 2)), ((1, 1), (3, 3)),
+        ((1, 3), (3, 1)), ((2, 2), (1, 0)), ((3, 0), (0, 1)), ((0, 3), (0, 0)),
     )
     x_codes = [sum(pair[i][0] * 4**g for g, pair in enumerate(offsets)) for i in range(2)]
     z_codes = [sum(pair[i][1] * 4**g for g, pair in enumerate(offsets)) for i in range(2)]

time: 40.8 us -> 40.9 us (level)
  no operation moved by 1% of the time
where the time goes in v6:
time: 40.9 us; the launch traced here: 40.7 us
  Pallas kernels  39.8 us (97%)
  local copies, waits for them, and re-layouts  0.97 us (2%)
    pallas_call x1, Pallas kernels, on_device(): pl.pallas_call(kernel, out_shape=jax.ShapeDtypeStruct((OUT,) + block, BF1...  39.8 us
    unnamed x1, local copies, waits for them, and re-layouts  0.97 us

profile of v6, /device:TPU:1, one launch (start us, length us, event | category | flops | bytes accessed | tf_op | source)
XLA Modules:
  0.0 40.7 jit_solution(16270514440472421484)
XLA Ops:
  0.0 39.8 %shard_map.91 = bf16[16,8,8,512]{3,2,1,0:T(8,128)(2,1)S(1)} custom-call(s32[1,8]{1,0:T(1,128)} %bitcast.17, s32[1,8]{1,0:T(1,128)} %bitcast.18, s32[1,32]{1,0:T(1,128)} %bitcast.19, s32[1,16]{1,0:T(1,128)} %bitcast.20, s32[27,1,32]{2,1,0:T(1,128)} %bitcast.15, s32[25,1,32]{2,1,0:T(1,128)} %bitcast.16, bf16[32,8,8,512]{3,2,1,0:T(8,128)(2,1)} %bitcast.14, ...), custom_call_target="tpu_custom_call" | custom-call | tf_op jit(solution)/shard_map/pallas_call | solution.py:432
  39.8 1.0 %copy.11 = bf16[1,1,16,8,8,512]{5,4,3,2,1,0:T(8,128)(2,1)} copy(bf16[1,1,16,8,8,512]{5,4,3,2,1,0:T(8,128)(2,1)S(1)} %bitcast.13) | data formatting | bytes 2097152
